TPU v7x, 256 devices: a whole 4x4x8 slice. The times are simulated.
256 devices in a mesh: tm: 64 (over y, z_hi, x), neur: 4 (over z_lo, core).
Axes of the slice: x: 4, y: 4, z: 8 (z_hi: 4, z_lo: 2; z = z_hi * 2 + z_lo), core: 2. Of those that a mesh axis runs over, the one named last changes fastest.
Arguments:
- recording: bfloat16 [2048, 16384], P('neur', 'tm'), may hold values from -6 to 6
- motifs: bfloat16 [128, 64, 2048], P(None, None, 'neur'), may hold values from -0.0625 to 0.0625
- loadings: bfloat16 [64, 16384], P(None, 'tm'), may hold values from -6 to 6
Outputs:
- grad_motifs: float32 [128, 64, 2048], P('tm', None, 'neur')
- grad_loadings: float32 [64, 16384], P(None, 'tm')
All inputs are finite; a program needn't handle non-finite values.
Results may differ from a plain program's by a relative error of at most 0.0021.
Values may be sent and summed in bfloat16 or wider, within the bound.
A program may use at most 128 MiB of HBM per device.

v0:
```python
import math

import jax
import jax.numpy as jnp
from jax import lax
from jax.sharding import PartitionSpec as P


def from_behind(block, axis, distance):
    devices = range(lax.axis_size(axis))
    route = [(i - distance, i) for i in devices if i - distance in devices]
    return lax.ppermute(block, axis, route)


def correlate(lhs, rhs, specs):
    return lax.conv_general_dilated(
        lhs, rhs, (1,), "VALID", dimension_numbers=specs, preferred_element_type=jnp.float32
    )


def forward_model(motifs, load_ext, time_len):
    reversed_load = load_ext[:, ::-1]
    result = correlate(reversed_load[None], motifs, ("NCH", "HIO", "NCH"))
    return result[0, :, :time_len][:, ::-1]


def backward_motif(motifs, res_ext, out_len):
    result = correlate(res_ext[None], motifs, ("NCH", "HOI", "NCH"))
    return result[0, :, :out_len]


def weight_term(reversed_load, reversed_res, piece_count):
    time_len = reversed_res.shape[1]
    window = lax.slice_in_dim(reversed_load, 0, piece_count + time_len - 1, axis=1)
    return correlate(window[:, None, :], reversed_res[:, None, :], ("NCH", "OIH", "HNC"))


def on_device(recording, motifs, loadings):
    lag_count = motifs.shape[0]
    motif_count = motifs.shape[1]
    neur_local = recording.shape[0]
    time_len = recording.shape[1]
    tm_count = lax.axis_size("tm")
    lag_share = lag_count // tm_count
    total_time = time_len * tm_count
    neurons = neur_local * lax.axis_size("neur")
    edge_cols = from_behind(loadings[:, time_len - lag_count :], "tm", 1)
    load_ext = jnp.concatenate([edge_cols, loadings], axis=1)
    rebuilt = forward_model(motifs, load_ext, time_len)
    residual = (rebuilt - recording.astype(jnp.float32)).astype(jnp.bfloat16)
    ahead_cols = from_behind(residual[:, :lag_count], "tm", -1)
    partial_value = backward_motif(
        motifs, jnp.concatenate([residual, ahead_cols], axis=1), time_len
    )
    grad_loadings = lax.psum(partial_value, "neur") * math.sqrt(motif_count / neurons)
    reversed_load = load_ext[:, ::-1]
    reversed_res = residual[:, ::-1]
    own_rows = lax.psum_scatter(
        weight_term(reversed_load, reversed_res, lag_share * lax.axis_size("tm")),
        "tm",
        scatter_dimension=0,
        tiled=True,
    )
    grad_motifs = own_rows * (1.0 / math.sqrt(total_time))
    return (grad_motifs, grad_loadings)


def solution(mesh):
    in_specs = (P("neur", "tm"), P(None, None, "neur"), P(None, "tm"))
    out_specs = (P("tm", None, "neur"), P(None, "tm"))
    return jax.shard_map(
        on_device, mesh=mesh, in_specs=in_specs, out_specs=out_specs, check_vma=False
    )
```

profile of v0, /device:TPU:0, one launch (start us, length us, event | category | flops | bytes accessed | tf_op | source)
XLA Modules:
  0.0 547.0 jit_solution(15876584063719561310)
XLA Ops:
  8.0 0.0 all-reduce.2.cloned.1.call-start
  8.0 0.7 slice.18
  8.8 1.7 collective-permute-start
  10.4 1.1 copy.6
  11.5 0.3 collective-permute-done
  11.9 0.8 constant_dynamic-update-slice_fusion
  12.6 0.3 rev.10
  12.9 0.1 slice.24
  13.0 0.2 copy.5
  13.2 18.7 %fusion.4 = f32[1,512,256]{1,0,2:T(1,128)S(1)} fusion(bf16[1,64,384]{1,0,2:T(2,128)(2,1)S(1)} %copy.5, bf16[128,64,512]{2,1,0:T(8,128)(2,1)} %param.4), kind=kOutput, calls=%fused_computation.12 | convolution fusion | flops 2147483648 | bytes 8962048 | tf_op jit(solution)/shard_map/slice | solution.py:24
  31.9 0.3 rev.11
  32.2 0.1 subtract_convert_fusion
  32.3 0.3 rev.12
  32.6 0.3 reverse.1
  32.9 1.5 collective-permute-start.1
  34.4 0.1 slice_bitcast_fusion
  34.4 0.2 copy.7
  34.6 5.4 collective-permute-done.1
  40.0 24.7 %fusion = f32[1,64,256]{1,0,2:T(1,128)} fusion(bf16[128,64,512]{2,1,0:T(8,128)(2,1)} %param.4, bf16[1,512,384]{1,2,0:T(8,128)(2,1)S(1)} %maximum_bitcast_fusion), kind=kOutput, calls=%fused_computation | convolution fusion | flops 2147483648 | bytes 8847360 | tf_op jit(solution)/shard_map/slice | solution.py:29
  64.7 0.0 all-reduce.2.cloned.1.call-update
  64.7 0.3 reduce-scatter.2.cloned.1.call-start
  65.0 19.4 %fusion.2 = f32[128,64,512]{2,1,0:T(8,128)} fusion(bf16[64,1,383]{0,1,2:T(2,128)(2,1)S(1)} %copy.7, bf16[512,1,256]{0,2,1:T(8,128)(2,1)S(1)} %bitcast.16), kind=kOutput, calls=%fused_computation.3 | convolution fusion | flops 2147483648 | bytes 17088384 | tf_op jit(solution)/shard_map/conv_general_dilated | solution.py:16
  84.4 0.0 reduce-scatter.2.cloned.1.call-update
  84.4 33.6 %all-reduce.2.cloned.1.call-done = f32[64,256]{0,1:T(8,128)} async-done(((f32[64,256]{0,1:T(8,128)}), f32[64,256]{0,1:T(8,128)}) %all-reduce.2.cloned.1.call-update) | async-done | bytes 65552 | tf_op jit(solution)/shard_map/psum | solution.py:55
  118.0 0.9 broadcast_multiply_fusion.1
  119.0 0.7 copy.10
  119.7 418.2 %reduce-scatter.2.cloned.1.call-done = f32[2,64,512]{2,1,0:T(8,128)} async-done(((f32[128,64,512]{2,1,0:T(8,128)}), f32[2,64,512]{2,1,0:T(8,128)}) %reduce-scatter.2.cloned.1.call-update) | async-done | bytes 262160 | tf_op jit(solution)/shard_map/reduce_scatter | solution.py:58
  537.9 1.7 broadcast_multiply_fusion
  (4 shorter events, 0.1 us)
Async XLA Ops:
  8.0 110.0 %all-reduce.2.cloned.1.call-start = ((), (), s32[]{:S(2)}) async-start(), calls=%async_computation.2 | async-start | bytes 262144 | tf_op jit(solution)/shard_map/psum | solution.py:55
  8.8 3.1 collective-permute-start
  32.9 7.1 %collective-permute-start.1 = (bf16[512,128]{0,1:T(8,128)(2,1)S(1)}, bf16[512,128]{0,1:T(8,128)(2,1)S(1)}, u32[]{:S(2)}, u32[]{:S(2)}) collective-permute-start(bf16[512,128]{0,1:T(8,128)(2,1)S(1)} %slice.25), channel_id=1, source_target_pairs={{4,0},{8,4},{12,8},{16,12},{20,16},{24,20},{28,24},{32,28},{36,32}... | collective-permute-start | bytes 393224 | tf_op jit(solution)/shard_map/ppermute | solution.py:12
  64.7 473.1 %reduce-scatter.2.cloned.1.call-start = ((), (), s32[]{:S(2)}) async-start(), calls=%async_computation.1 | async-start | bytes 17039360 | tf_op jit(solution)/shard_map/reduce_scatter | solution.py:58
Sparse Core Ops, SparseCore 0:
  64.9 53.1 all-reduce.1
Sparse Core Ops, SparseCore 1:
  84.5 453.3 reduce-scatter.1
where the time goes:
time: 547 us
  waiting for transfers between devices  458 us (84%)
  matrix products  62.7 us (11%)
  between operations  15.6 us (3%)
    reduce_scatter x1, waiting for transfers between devices, on_device(): lax.psum_scatter(weight_term(reversed_load, reversed_res, lag_share * lax...  418 us
    psum x1, waiting for transfers between devices, on_device(): lax.psum(partial_value, 'neur') * math.sqrt(motif_count / neurons)  33.6 us
    slice x1, matrix products, backward_motif(): return result[0, :, :out_len]  24.7 us
    conv_general_dilated x1, matrix products, correlate(): lax.conv_general_dilated(lhs, rhs, (1,), 'VALID', dimension_numbers=specs...  19.4 us
    slice x1, matrix products, forward_model(): return result[0, :, :time_len][:, ::-1]  18.7 us
  transfers between devices with their start and end apart: 4, of which 4 were waited for; matrix products, arithmetic and copies ran while one was open for 4% of the time, Pallas kernels for 0%

commit v1 on v0

v1 whole, which is shorter than its diff:
```python
import functools
import math

import jax
import jax.numpy as jnp
from jax import lax
from jax.experimental import pallas as pl
from jax.experimental.pallas import tpu as pltpu
from jax.sharding import PartitionSpec as P

F32 = jnp.float32
BF16 = jnp.bfloat16
NX = NY = NZ = 4
LAGS, K, N, T = 128, 64, 512, 256
J = 16
M = LAGS // J
Q = 256
OFFS = [32 * dy + 8 * pz + b for dy in range(2) for pz in range(NZ) for b in range(2)]


def kernel(
    glscale, gmscale, rec_hbm, w_hbm, load_hbm, gm_ref, gl_ref,
    rec_v, w_v, hext, hal, htp, x16, reb, rt, hb, rb, a_v, acc, p_v,
    gp, gr, gs, gh, glb, sz, zb, zf,
    load_sem, rec_sem, w_sem, hal_sem, send_sem, recv_sem, g_sem, g2_sem, z_send, z_recv, self_sem,
):
    tm = lax.axis_index("tm")
    ne = lax.axis_index("neur")
    tms = NX * NY * NZ
    x, zh, y = lax.rem(tm, NX), lax.rem(lax.div(tm, NX), NZ), lax.div(tm, NX * NZ)
    zl, c = lax.div(ne, 2), lax.rem(ne, 2)

    def dev(xx, yy, zz, ll, cc):
        return {"tm": (yy * NZ + zz) * NX + xx, "neur": ll * 2 + cc}

    def rc(src, dst, ssem, rsem, target):
        return pltpu.make_async_remote_copy(
            src_ref=src, dst_ref=dst, send_sem=ssem, recv_sem=rsem,
            device_id=target, device_id_type=pl.DeviceIdType.MESH,
        )

    def add(value, step, size):
        return lax.rem(value + step, size)

    own_cp = pltpu.make_async_copy(load_hbm, hext.at[:, pl.ds(128, T)], load_sem)
    own_cp.start()
    rec_cp = pltpu.make_async_copy(rec_hbm, rec_v, rec_sem)
    rec_cp.start()
    for m in range(M):
        pltpu.make_async_copy(w_hbm.at[m], w_v.at[m], w_sem.at[m]).start()

    barrier = pltpu.get_barrier_semaphore()
    greet = []
    for dy in range(NY):
        for dz in range(NZ):
            for dc in range(2):
                if dy or dz or dc:
                    greet.append(dev(x, add(y, dy, NY), add(zh, dz, NZ), zl, add(c, dc, 2)))
    for dx in (1, NX - 1):
        greet.append(dev(add(x, dx, NX), y, zh, zl, c))
    for dt in (1, tms - 1):
        greet.append({"tm": add(tm, dt, tms), "neur": ne})
    for dc in range(2):
        greet.append(dev(x, y, zh, 1 - zl, add(c, dc, 2)))
    for target in greet:
        pl.semaphore_signal(barrier, inc=1, device_id=target, device_id_type=pl.DeviceIdType.MESH)

    sends = []

    own_cp.wait()

    def build_htp(first):
        block = hext[:, first : first + 256].astype(F32)
        pair = jnp.concatenate([block, pltpu.roll(block, 1, 1)], axis=0)
        htp[first : first + 256] = pair.T

    def build_x16(first, rows):
        for p in range(J // 2):
            x16[pl.ds(first, rows), 128 * p : 128 * (p + 1)] = htp[
                first - 2 * p : first - 2 * p + rows
            ].astype(BF16)

    build_htp(128)
    build_x16(144, 240)
    reb[...] = jnp.zeros_like(reb)

    def forward(half, waits):
        def body(m, carry):
            if waits:
                pltpu.make_async_copy(w_hbm.at[m], w_v.at[m], w_sem.at[m]).wait()
            first = pl.multiple_of(128 + 128 * half - J * m, J)
            reb[pl.ds(128 * half, 128)] += jnp.dot(
                x16[pl.ds(first, 128)], w_v[m], preferred_element_type=F32
            )
            return carry

        lax.fori_loop(0, M, body, 0)
        rows = slice(128 * half, 128 * half + 128)
        rt[rows] = (reb[rows] - rec_v[:, rows].astype(F32).T).astype(BF16)

    forward_hi = functools.partial(forward, 1, True)

    pl.semaphore_wait(barrier, len(greet))
    halo = rc(
        hext.at[:, pl.ds(256, 128)], hal, hal_sem.at[0], hal_sem.at[1],
        {"tm": add(tm, 1, tms), "neur": ne},
    )
    halo.start()
    sends.append(halo)
    rec_cp.wait()
    forward_hi()

    def slot(q, kk, xs, i):
        if q == 0:
            return hb.at[(kk * NX + xs) * 2 + i]
        return rb.at[kk * NX + xs, pl.ds(pl.multiple_of(i * 256 + (q - 1) * 128, 128), 128)]

    def landed(q, kk, xs, i):
        return recv_sem.at[q, (kk * NX + xs) * 2 + i]

    def await_slot(q, kk, xs, i):
        ref = slot(q, kk, xs, i)
        rc(ref, ref, send_sem.at[q, 0], landed(q, kk, xs, i), dev(x, y, zh, zl, 1 - c)).wait_recv()

    def pass_on(q, kk, xs, i, number, target):
        ref = slot(q, kk, xs, i)
        copy = rc(ref, ref, send_sem.at[q, number], landed(q, kk, xs, i), target)
        copy.start()
        sends.append(copy)

    right = dev(add(x, 1, NX), y, zh, zl, c)
    left = dev(add(x, NX - 1, NX), y, zh, zl, c)
    sibling = dev(x, y, zh, zl, 1 - c)
    par, half_y = lax.rem(y, 2), lax.div(y, 2)
    y_waits = []

    def to_row(q):
        for h in range(2):
            if q == 0:
                src = hext
            else:
                src = rt.at[pl.ds(128 * (q - 1), 128), pl.ds(Q * h, Q)]
            dst = slot(q, par, x, half_y)
            sem = landed(q, par, x, half_y)
            remote = rc(src, dst, send_sem.at[q, h], sem, dev(x, 2 * c + h, zh, zl, par))
            local = pltpu.make_async_copy(src, dst, sem)
            is_self = jnp.logical_and(y == 2 * c + h, c == par)

            @pl.when(is_self)
            def _():
                local.start()

            @pl.when(jnp.logical_not(is_self))
            def _():
                remote.start()

            y_waits.append((is_self, remote))

    def hop0(q):
        for i in range(2):
            await_slot(q, c, x, i)
            pass_on(q, c, x, i, 2 + i, right)
            pass_on(q, c, x, i, 4 + i, left)
            pass_on(q, c, x, i, 6 + i, sibling)

    def hop1(q):
        xl, xr = add(x, NX - 1, NX), add(x, 1, NX)
        await_slot(q, c, xl, 0)
        pass_on(q, c, xl, 0, 8, right)
        pass_on(q, c, xl, 0, 9, sibling)
        await_slot(q, c, xr, 1)
        pass_on(q, c, xr, 1, 10, left)
        pass_on(q, c, xr, 1, 11, sibling)
        await_slot(q, c, xl, 1)
        pass_on(q, c, xl, 1, 12, sibling)
        await_slot(q, c, xr, 0)
        pass_on(q, c, xr, 0, 13, sibling)

    def hop2(q):
        xo = add(x, 2, NX)
        for i in range(2):
            await_slot(q, c, xo, i)
            pass_on(q, c, xo, i, 14 + i, sibling)

    def hop3(q, dx):
        for i in range(2):
            await_slot(q, 1 - c, add(x, dx, NX), i)

    to_row(2)
    halo.wait_recv()
    hext[:, 0:128] = jnp.where(tm == 0, jnp.zeros_like(hal[...], F32), hal[...].astype(F32)).astype(BF16)
    build_htp(0)
    build_x16(16, 128)
    to_row(0)
    forward(0, False)
    to_row(1)
    hop0(0)
    hop0(2)

    p_v[...] = jnp.zeros_like(p_v)

    def back(first, last):
        def body(m, carry):
            rows = pl.ds(pl.multiple_of(128 - J * m, J), T)
            p_v[rows] += lax.dot_general(
                rt[...], w_v[m], (((1,), (1,)), ((), ())), preferred_element_type=F32
            )
            return carry

        lax.fori_loop(first, last, body, 0)

    back(0, M // 2)
    hop0(1)
    hop1(0)
    hop1(2)
    back(M // 2, M)
    hop1(1)
    hop2(0)
    hop2(2)

    even = jnp.zeros((384, 128), F32)
    odd = jnp.zeros((384, 128), F32)
    for p in range(J // 2):
        lanes = slice(128 * p, 128 * (p + 1))
        even += p_v[2 * p : 2 * p + 384, lanes]
        odd += p_v[2 * p + 1 : 2 * p + 385, lanes]
    gp[...] = (even + pltpu.roll(odd, 64, 1)).T[0:K]

    def neur_at(d):
        return {"tm": tm, "neur": add(ne, d, 4)}

    for d in range(1, 4):
        rows = pl.ds(pl.multiple_of(add(ne, d, 4) * 16, 16), 16)
        copy = rc(gp.at[rows], gr.at[d - 1], g_sem.at[0, d - 1], g_sem.at[1, d - 1], neur_at(d))
        copy.start()
        sends.append(copy)
    hop2(1)

    for dx in range(NX):
        hop3(0, dx)
    base = 64 * c + 2 * x

    def build_a(idx, carry):
        rolled = pltpu.roll(hb[idx].astype(F32), base, 1)
        kx, i = lax.div(idx, 2), lax.rem(idx, 2)
        cols = pl.ds(pl.multiple_of(i * T, T), T)
        for o, off in enumerate(OFFS):
            moved = pltpu.roll(rolled, off, 1) if off else rolled
            a_v[kx, K * o : K * (o + 1), cols] = moved[:, 128:384].astype(BF16)
        return carry

    lax.fori_loop(0, 2 * 2 * NX, build_a, 0)

    mine = pl.ds(pl.multiple_of(ne * 16, 16), 16)
    total = gp[mine]
    for d in range(1, 4):
        rc(gr.at[d - 1], gr.at[d - 1], g_sem.at[0, d - 1], g_sem.at[1, d - 1], neur_at(d)).wait_recv()
        total += gr[d - 1]
    gs[...] = total
    edge = rc(
        gs.at[:, pl.ds(0, 128)], gh, g_sem.at[0, 3], g_sem.at[1, 3],
        {"tm": add(tm, tms - 1, tms), "neur": ne},
    )
    edge.start()
    sends.append(edge)

    order = [(c, add(x, dx, NX)) for dx in (0, 1, 3, 2)] + [(1 - c, add(x, dx, NX)) for dx in (0, 1, 3, 2)]
    dxs = (0, 1, 3, 2)
    for step, (kk, xs) in enumerate(order):
        if step >= 4:
            hop3(2, dxs[step - 4])
            hop3(1, dxs[step - 4])
        kx = kk * NX + xs
        part = jnp.dot(a_v[kx], rb[kx], preferred_element_type=F32)
        if step == 0:
            acc[...] = part
        else:
            acc[...] += part
        if step == 3:
            edge.wait_recv()
            last = gh[...]
            own = gs[:, 128:384]
            rest = jnp.where(tm == tms - 1, jnp.zeros_like(last), last)
            glb[mine] = (own + jnp.concatenate([jnp.zeros_like(last), rest], axis=1)) * glscale
            for d in range(1, 4):
                copy = rc(glb.at[mine], glb.at[mine], g2_sem.at[0, d - 1], g2_sem.at[1, d - 1], neur_at(d))
                copy.start()
                sends.append(copy)

    z_waits = []
    for dz in (2, 1, 3, 0):
        pz = add(zh, dz, NZ)
        for dy in range(2):
            rows = pl.ds(pl.multiple_of((dy * NZ + pz) * 128, 128), 128)
            target = dev(x, 2 * c + dy, pz, zl, half_y)
            if dz:
                sz[dy, dz - 1] = acc[rows].astype(BF16)
                copy = rc(
                    sz.at[dy, dz - 1], zb.at[par, dz - 1], z_send.at[dy, dz], z_recv.at[par, dz], target
                )
                copy.start()
                sends.append(copy)
            else:
                remote = rc(acc.at[rows], zf.at[par], z_send.at[dy, 0], z_recv.at[par, 0], target)
                local = pltpu.make_async_copy(acc.at[rows], zf.at[par], z_recv.at[par, 0])
                is_self = jnp.logical_and(half_y == c, par == dy)

                @pl.when(is_self)
                def _():
                    local.start()

                @pl.when(jnp.logical_not(is_self))
                def _():
                    remote.start()

                z_waits.append((is_self, remote))

    for d in range(1, 4):
        rows = pl.ds(pl.multiple_of(add(ne, 4 - d, 4) * 16, 16), 16)
        rc(glb.at[rows], glb.at[rows], g2_sem.at[0, d - 1], g2_sem.at[1, d - 1], neur_at(d)).wait_recv()
    gl_ref[...] = glb[...]

    for h in range(2):
        rc(zf.at[h], zf.at[h], z_send.at[0, 0], z_recv.at[h, 0], sibling).wait_recv()
        value = zf[h]
        for dz in (1, 3, 2):
            rc(zb.at[h, dz - 1], zb.at[h, dz - 1], z_send.at[0, dz], z_recv.at[h, dz], sibling).wait_recv()
            value += zb[h, dz - 1].astype(F32)
        value = value * gmscale
        for b in range(2):
            gm_ref[b, :, Q * h : Q * (h + 1)] = value[K * b : K * (b + 1)]

    for copy in sends:
        copy.wait_send()
    for is_self, copy in y_waits + z_waits:

        @pl.when(jnp.logical_not(is_self))
        def _():
            copy.wait_send()


def on_device(recording, motifs, loadings):
    neurons = recording.shape[0] * lax.axis_size("neur")
    total_time = recording.shape[1] * lax.axis_size("tm")
    glscale = math.sqrt(motifs.shape[1] / neurons)
    gmscale = 1.0 / math.sqrt(total_time)
    vm = pltpu.VMEM
    dma = pltpu.SemaphoreType.DMA
    return pl.pallas_call(
        functools.partial(kernel, glscale, gmscale),
        out_shape=(
            jax.ShapeDtypeStruct((2, K, N), F32),
            jax.ShapeDtypeStruct((K, T), F32),
        ),
        in_specs=[pl.BlockSpec(memory_space=pl.ANY)] * 3,
        out_specs=(pl.BlockSpec(memory_space=pltpu.VMEM),) * 2,
        scratch_shapes=[
            vm((N, T), BF16),
            vm((M, J * K, N), BF16),
            vm((K, 384), BF16),
            vm((K, 128), BF16),
            vm((384, 128), F32),
            vm((384, J * K), BF16),
            vm((T, N), F32),
            vm((T, N), BF16),
            vm((16, K, 384), BF16),
            vm((8, 2 * T, Q), BF16),
            vm((8, J * K, 2 * T), BF16),
            vm((J * K, Q), F32),
            vm((400, J * K), F32),
            vm((K, 384), F32),
            vm((3, 16, 384), F32),
            vm((16, 384), F32),
            vm((16, 128), F32),
            vm((K, T), F32),
            vm((2, 3, 128, Q), BF16),
            vm((2, 3, 128, Q), BF16),
            vm((2, 128, Q), F32),
            dma, dma, dma((M,)), dma((2,)), dma((3, 16)), dma((3, 16)), dma((2, 4)), dma((2, 3)),
            dma((2, 4)), dma((2, 4)), dma,
        ],
        compiler_params=pltpu.CompilerParams(
            collective_id=0, has_side_effects=True, vmem_limit_bytes=60 * 1024 * 1024
        ),
    )(recording, motifs.reshape(M, J * K, N), loadings)


def solution(mesh):
    in_specs = (P("neur", "tm"), P(None, None, "neur"), P(None, "tm"))
    out_specs = (P("tm", None, "neur"), P(None, "tm"))
    return jax.shard_map(
        on_device, mesh=mesh, in_specs=in_specs, out_specs=out_specs, check_vma=False
    )
```

time: 547 us -> 63.3 us (0.12)
  the two profiles are of different devices: /device:TPU:0 before, /device:TPU:14 now
where the time goes in v1:
time: 63.3 us; the launch traced here: 63.1 us
  Pallas kernels  59.3 us (94%)
  local copies, waits for them, and re-layouts  3.14 us (5%)
  between operations  0.64 us (1%)
    pallas_call x1, Pallas kernels, on_device(): pl.pallas_call(functools.partial(kernel, glscale, gmscale), out_shape=(ja...  59.3 us
    unnamed x2, local copies, waits for them, and re-layouts  3.14 us

profile of v1, /device:TPU:14, one launch (start us, length us, event | category | flops | bytes accessed | tf_op | source)
XLA Modules:
  0.0 63.1 jit_solution(3187581940281905434)
XLA Ops:
  0.6 59.3 %shard_map.50 = (f32[2,64,512]{2,1,0:T(8,128)}, f32[64,256]{1,0:T(8,128)}) custom-call(bf16[512,256]{1,0:T(8,128)(2,1)} %rec_hbm.1, bf16[8,1024,512]{2,1,0:T(8,128)(2,1)} %bitcast.1, bf16[64,256]{1,0:T(8,128)(2,1)} %load_hbm.1), custom_call_target="tpu_custom_call" | custom-call | tf_op jit(solution)/shard_map/pallas_call | solution.py:349
  60.0 1.7 %copy.7 = f32[2,64,512]{2,1,0:T(8,128)} copy(f32[2,64,512]{2,1,0:T(8,128)} %get-tuple-element.4) | data formatting | bytes 524288
  61.6 1.5 %copy.8 = f32[64,256]{1,0:T(8,128)} copy(f32[64,256]{1,0:T(8,128)} %get-tuple-element.5) | data formatting | bytes 131072
